TPU v7x, 128 devices: a whole 4x4x4 slice. The times are simulated.
128 devices in a mesh: expert: 8 (over z_lo, x), shard: 16 (over z_hi, y, core).
Axes of the slice: x: 4, y: 4, z: 4 (z_hi: 2, z_lo: 2; z = z_hi * 2 + z_lo), core: 2. Of those that a mesh axis runs over, the one named last changes fastest.
Arguments:
- tokens: bfloat16 [1024, 4096], P('expert', 'shard'), may hold values from -6 to 6
- routes: int32 [1024, 2], P('expert'), may hold values from 0 to 7, all different within a row; in each aligned block of 128 rows (0 to 127, 128 to 255, ...) at most 96 rows name the same one
- mix_weights: float32 [1024, 2], P('expert'), may hold values from 0.1 to 1
- cotangent: bfloat16 [1024, 4096], P('expert', 'shard'), may hold values from -6 to 6
- w_gate: bfloat16 [8, 4096, 6144], P('expert', 'shard'), may hold values from -0.09375 to 0.09375
- w_up: bfloat16 [8, 4096, 6144], P('expert', 'shard'), may hold values from -0.09375 to 0.09375
- w_down: bfloat16 [8, 4096, 6144], P('expert', 'shard'), may hold values from -0.078125 to 0.078125
Outputs:
- layer_out: bfloat16 [1024, 4096], P('expert', 'shard')
- grad_tokens: bfloat16 [1024, 4096], P('expert', 'shard')
- grad_gate: bfloat16 [8, 4096, 6144], P('expert', None, 'shard')
- grad_up: bfloat16 [8, 4096, 6144], P('expert', None, 'shard')
- grad_down: bfloat16 [8, 4096, 6144], P('expert', None, 'shard')
Inputs may be any that keep to these rules, and one draw needn't show every extreme that they name: `routes`: each token names two different experts. Among the 128 tokens of one block, no expert is named by more than 96 tokens, and in every draw some expert is named by exactly 96 tokens of some block. Every expert is named by some token.
All inputs are finite; a program needn't handle non-finite values.
Results may differ from a plain program's by a relative error of at most 0.015.
Values may be sent and summed in bfloat16 or wider, within the bound.
No kernel may reach another device: no remote copies, remote signals or barrier semaphores. Data moves between devices by JAX's collectives and lax.ppermute only.
A program may use at most 128 MiB of HBM per device.

v0:
```python
import jax
import jax.numpy as jnp
from jax import lax
from jax.sharding import PartitionSpec as P


def slot_targets(routes, capacity, experts):
    flat_routes = routes.reshape(-1)
    expert_iota = jnp.arange(experts, dtype=jnp.int32)
    one_hot = (flat_routes[:, None] == expert_iota[None, :]).astype(jnp.int32)
    earlier = jnp.cumsum(one_hot, axis=0) - one_hot
    slot_number = jnp.sum(earlier * one_hot, axis=1)
    return (flat_routes * capacity + slot_number).reshape(routes.shape)


def feature_total(partial_value):
    return lax.psum_scatter(
        partial_value.astype(jnp.bfloat16), "shard", scatter_dimension=1, tiled=True
    )


def send_home(row_block, experts, capacity):
    shaped = row_block.reshape(experts, capacity, row_block.shape[1])
    returned = lax.all_to_all(shaped, "expert", split_axis=0, concat_axis=0, tiled=True)
    return returned.reshape(experts * capacity, row_block.shape[1])


def local(tokens, routes, mix_weights, cotangent, w_gate, w_up, w_down):
    experts = lax.axis_size("expert")
    tok_dev = tokens.shape[0]
    capacity = min(tok_dev, 6 * tok_dev // experts)
    target = slot_targets(routes, capacity, experts)
    slot_iota = jnp.arange(experts * capacity, dtype=jnp.int32)
    slot_hits = slot_iota[:, None, None] == target[None, :, :]
    picker = jnp.sum(slot_hits.astype(jnp.float32), axis=2).astype(jnp.bfloat16)
    slot_weight = jnp.sum(jnp.where(slot_hits, mix_weights[None, :, :], 0.0), axis=(1, 2))
    gate_own, up_own, down_own = (
        lax.all_to_all(w_gate, "shard", split_axis=2, concat_axis=1, tiled=True),
        lax.all_to_all(w_up, "shard", split_axis=2, concat_axis=1, tiled=True),
        lax.all_to_all(w_down, "shard", split_axis=2, concat_axis=1, tiled=True),
    )
    gate_own = gate_own[0]
    up_own = up_own[0]
    down_own = down_own[0]
    piece_width = tokens.shape[1]
    row_send = jnp.dot(picker, tokens, preferred_element_type=jnp.float32).astype(jnp.bfloat16)
    grad_send = (
        jnp.dot(picker, cotangent, preferred_element_type=jnp.float32) * slot_weight[:, None]
    ).astype(jnp.bfloat16)
    row_send = row_send.reshape(experts, capacity, piece_width)
    grad_send = grad_send.reshape(experts, capacity, piece_width)
    row_part, grad_part = (
        lax.all_to_all(row_send, "expert", split_axis=0, concat_axis=0, tiled=True),
        lax.all_to_all(grad_send, "expert", split_axis=0, concat_axis=0, tiled=True),
    )
    row_recv, grad_recv = (
        lax.all_gather(row_part, "shard", axis=2, tiled=True),
        lax.all_gather(grad_part, "shard", axis=2, tiled=True),
    )
    model_width = row_recv.shape[2]
    x_rows = row_recv.reshape(-1, model_width)
    dy_rows = grad_recv.reshape(-1, model_width)
    gate_pre = jnp.dot(x_rows, gate_own, preferred_element_type=jnp.float32)
    up_pre = jnp.dot(x_rows, up_own, preferred_element_type=jnp.float32)
    sigmoid_gate = jax.nn.sigmoid(gate_pre)
    active = gate_pre * sigmoid_gate
    hidden = (active * up_pre).astype(jnp.bfloat16)
    down_part = lax.dot_general(
        hidden, down_own, (((1,), (1,)), ((), ())), preferred_element_type=jnp.float32
    )
    out_home = send_home(feature_total(down_part), experts, capacity)
    picked = out_home[target]
    layer_out = jnp.sum(mix_weights[:, :, None] * picked.astype(jnp.float32), axis=1).astype(
        jnp.bfloat16
    )
    d_hidden = jnp.dot(dy_rows, down_own, preferred_element_type=jnp.float32)
    d_gate = (d_hidden * up_pre * sigmoid_gate * (1.0 + gate_pre * (1.0 - sigmoid_gate))).astype(
        jnp.bfloat16
    )
    d_up = (d_hidden * active).astype(jnp.bfloat16)
    row_contract = (((0,), (0,)), ((), ()))
    grad_down = lax.dot_general(
        dy_rows, hidden, row_contract, preferred_element_type=jnp.float32
    ).astype(jnp.bfloat16)
    grad_gate = lax.dot_general(
        x_rows, d_gate, row_contract, preferred_element_type=jnp.float32
    ).astype(jnp.bfloat16)
    grad_up = lax.dot_general(
        x_rows, d_up, row_contract, preferred_element_type=jnp.float32
    ).astype(jnp.bfloat16)
    col_contract = (((1,), (1,)), ((), ()))
    dx_part = lax.dot_general(d_gate, gate_own, col_contract, preferred_element_type=jnp.float32)
    dx_part = dx_part + lax.dot_general(
        d_up, up_own, col_contract, preferred_element_type=jnp.float32
    )
    dx_home = send_home(feature_total(dx_part), experts, capacity)
    grad_tokens = jnp.sum(dx_home[target].astype(jnp.float32), axis=1).astype(jnp.bfloat16)
    return (layer_out, grad_tokens, grad_gate[None], grad_up[None], grad_down[None])


def solution(mesh):
    return jax.shard_map(
        local,
        mesh=mesh,
        in_specs=(
            P("expert", "shard"),
            P("expert", None),
            P("expert", None),
            P("expert", "shard"),
            P("expert", "shard", None),
            P("expert", "shard", None),
            P("expert", "shard", None),
        ),
        out_specs=(
            P("expert", "shard"),
            P("expert", "shard"),
            P("expert", None, "shard"),
            P("expert", None, "shard"),
            P("expert", None, "shard"),
        ),
        check_vma=False,
    )
```

profile of v0, /device:TPU:2, one launch (start us, length us, event | category | flops | bytes accessed | tf_op | source)
XLA Modules:
  0.0 506.1 jit_solution(3655186438694341094)
XLA Ops:
  7.2 0.9 copy.58
  8.2 0.1 eq.43
  8.3 0.1 eq.39
  8.5 0.6 reduce-window.6
  9.1 0.2 slice_reduce_fusion
  9.3 0.1 fusion.8
  9.4 0.1 reduce_sum.51
  9.6 0.1 copy.60
  9.6 0.7 compare_select_fusion
  10.3 0.9 select_reduce_fusion
  11.2 0.2 convolution_convert_fusion.4
  11.5 13.6 %all_to_all.65 = bf16[8,96,256]{2,1,0:T(8,128)(2,1)} all-to-all(bf16[8,96,256]{2,1,0:T(8,128)(2,1)S(1)} %bitcast.80), channel_id=1, replica_groups=mesh['expert'=8,'shard'=16] {'expert'}, dimensions={0} | all-to-all | bytes 786432 | tf_op jit(solution)/shard_map/all_to_all | solution.py:53
  25.1 1.1 fusion.3
  26.2 11.2 %all_to_all.66 = bf16[8,96,256]{2,1,0:T(8,128)(2,1)} all-to-all(bf16[8,96,256]{2,1,0:T(8,128)(2,1)S(1)} %bitcast.79), channel_id=1, replica_groups=mesh['expert'=8,'shard'=16] {'expert'}, dimensions={0} | all-to-all | bytes 786432 | tf_op jit(solution)/shard_map/all_to_all | solution.py:54
  37.5 10.5 %copy.61 = bf16[1,256,6144]{1,0,2:T(2,128)(2,1)} copy(bf16[1,256,6144]{2,1,0:T(8,128)(2,1)S(1)} %copy-done.4) | data formatting | bytes 6291456 | tf_op args[4]
  48.0 0.5 broadcast.52
  48.5 31.5 %reduce.4 = bf16[6144,256]{1,0:T(8,128)(2,1)S(1)} reduce(bf16[6144,1,256]{2,1,0:T(2,128)(2,1)} %bitcast.62, bf16[]{:T(256)} %broadcast.52), dimensions={1}, to_apply=%bitcast.36.reduce_sub_computation | reduce | bytes 6291458
  80.0 3.5 reshape.99
  83.5 7.6 %all-to-all-start.1 = ((bf16[16,2,49152]{2,1,0:T(2,128)(2,1)}), bf16[16,2,49152]{2,1,0:T(2,128)(2,1)S(1)}, u32[]{:S(2)}, u32[]{:S(2)}) async-start(bf16[16,2,49152]{2,1,0:T(2,128)(2,1)} %reshape.99), calls=%async_computation.1 | async-start | bytes 6291456 | tf_op jit(solution)/shard_map/all_to_all | solution.py:38
  91.1 14.0 %copy.63 = bf16[1,256,6144]{1,0,2:T(2,128)(2,1)} copy(bf16[1,256,6144]{2,1,0:T(8,128)(2,1)} %param.12) | data formatting | bytes 6291456 | tf_op args[5]
  105.1 33.2 %reduce.5 = bf16[6144,256]{1,0:T(8,128)(2,1)} reduce(bf16[6144,1,256]{2,1,0:T(2,128)(2,1)} %bitcast.67, bf16[]{:T(256)} %broadcast.52), dimensions={1}, to_apply=%bitcast.34.reduce_sub_computation | reduce | bytes 6291458
  138.3 6.3 %reshape.97 = bf16[16,2,49152]{2,1,0:T(2,128)(2,1)} reshape(bf16[6144,256]{1,0:T(8,128)(2,1)} %reduce.5) | data formatting | bytes 6291456
  144.6 7.7 %all-to-all-start.2 = ((bf16[16,2,49152]{2,1,0:T(2,128)(2,1)}), bf16[16,2,49152]{2,1,0:T(2,128)(2,1)}, u32[]{:S(2)}, u32[]{:S(2)}) async-start(bf16[16,2,49152]{2,1,0:T(2,128)(2,1)} %reshape.97), calls=%async_computation.2 | async-start | bytes 6291456 | tf_op jit(solution)/shard_map/all_to_all | solution.py:39
  152.4 14.0 %copy.65 = bf16[1,256,6144]{1,0,2:T(2,128)(2,1)} copy(bf16[1,256,6144]{2,1,0:T(8,128)(2,1)} %param.13) | data formatting | bytes 6291456 | tf_op args[6]
  166.4 33.2 %reduce.6 = bf16[6144,256]{1,0:T(8,128)(2,1)} reduce(bf16[6144,1,256]{2,1,0:T(2,128)(2,1)} %bitcast.63, bf16[]{:T(256)} %broadcast.52), dimensions={1}, to_apply=%bitcast.38.reduce_sub_computation | reduce | bytes 6291458
  199.6 6.4 %reshape.101 = bf16[16,2,49152]{2,1,0:T(2,128)(2,1)} reshape(bf16[6144,256]{1,0:T(8,128)(2,1)} %reduce.6) | data formatting | bytes 6291456
  206.0 7.4 %all-to-all-start.3 = ((bf16[16,2,49152]{2,1,0:T(2,128)(2,1)}), bf16[16,2,49152]{2,1,0:T(2,128)(2,1)}, u32[]{:S(2)}, u32[]{:S(2)}) async-start(bf16[16,2,49152]{2,1,0:T(2,128)(2,1)} %reshape.101), calls=%async_computation.3 | async-start | bytes 6291456 | tf_op jit(solution)/shard_map/all_to_all | solution.py:40
  213.4 7.7 %reshape.100 = bf16[6144,1,256]{2,1,0:T(2,128)(2,1)} reshape(bf16[16,2,49152]{2,1,0:T(2,128)(2,1)S(1)} %all-to-all-done.1) | data formatting | bytes 6291456
  221.1 3.3 copy.68
  224.4 2.8 copy.62
  227.2 11.5 %reshape.98 = bf16[6144,1,256]{2,1,0:T(2,128)(2,1)} reshape(bf16[16,2,49152]{2,1,0:T(2,128)(2,1)} %all-to-all-done.2) | data formatting | bytes 6291456
  238.6 3.3 copy.69
  242.0 2.8 copy.64
  244.7 10.9 %all-to-all-done.3 = bf16[16,2,49152]{2,1,0:T(2,128)(2,1)} async-done(((bf16[16,2,49152]{2,1,0:T(2,128)(2,1)}), bf16[16,2,49152]{2,1,0:T(2,128)(2,1)}, u32[]{:S(2)}, u32[]{:S(2)}) %all-to-all-start.3) | async-done | bytes 3145760 | tf_op jit(solution)/shard_map/all_to_all | solution.py:40
  255.7 11.5 %reshape.102 = bf16[6144,1,256]{2,1,0:T(2,128)(2,1)} reshape(bf16[16,2,49152]{2,1,0:T(2,128)(2,1)} %all-to-all-done.3) | data formatting | bytes 6291456
  267.1 3.3 copy.70
  270.4 2.8 copy.66
  273.2 8.3 %fusion.10 = f32[768,384]{1,0:T(8,128)} fusion(bf16[768,4096]{1,0:T(8,128)(2,1)} %bitcast.83, bf16[4096,384]{1,0:T(8,128)(2,1)} %bitcast.71), kind=kOutput, calls=%fused_computation.34 | convolution fusion | flops 2415919104 | bytes 10616832 | tf_op jit(solution)/shard_map/dot_general | solution.py:63
  281.6 4.4 fusion.11
  286.0 8.2 %multiply_convert_fusion = (bf16[768,384]{1,0:T(8,128)(2,1)}, bf16[768,384]{1,0:T(8,128)(2,1)}, bf16[768,384]{1,0:T(8,128)(2,1)S(1)}) fusion(f32[768,384]{1,0:T(8,128)} %fusion.10, f32[768,384]{1,0:T(8,128)} %fusion.11, bf16[768,4096]{1,0:T(8,128)(2,1)} %bitcast.87, bf16[4096,384]{1,0:T(8,128)(2,1)S(1)} %bitcast.77), kind=kOutput, calls=%fused_computation.13 | convolution fusion | flops 2420342784 | bytes 13565952 | tf_op jit(solution)/shard_map/dot_general | solution.py:76
  294.2 0.9 copy-done.9
  295.1 5.4 %convolution_convert_fusion = bf16[768,4096]{1,0:T(8,128)(2,1)} fusion(bf16[768,384]{1,0:T(8,128)(2,1)S(1)} %get-tuple-element.11, bf16[4096,384]{1,0:T(8,128)(2,1)S(1)} %bitcast.78), kind=kOutput, calls=%fused_computation.3 | convolution fusion | flops 2419064832 | bytes 10027008 | tf_op jit(solution)/shard_map/dot_general | solution.py:68
  300.5 0.2 reduce-scatter.5.cloned.1.call-start
  300.7 0.8 copy-done.5
  301.5 5.4 %fusion.12 = f32[768,4096]{1,0:T(8,128)S(1)} fusion(bf16[768,384]{1,0:T(8,128)(2,1)S(1)} %copy-done.5, bf16[4096,384]{1,0:T(8,128)(2,1)} %bitcast.72), kind=kOutput, calls=%fused_computation.36 | convolution fusion | flops 2415919104 | bytes 16318464 | tf_op jit(solution)/shard_map/dot_general | solution.py:92
  306.9 7.4 %add_convert_fusion = bf16[768,4096]{1,0:T(8,128)(2,1)} fusion(f32[768,4096]{1,0:T(8,128)S(1)} %fusion.12, bf16[768,384]{1,0:T(8,128)(2,1)S(1)} %copy-done.6, bf16[4096,384]{1,0:T(8,128)(2,1)} %bitcast.73), kind=kOutput, calls=%fused_computation.2 | convolution fusion | flops 2422210560 | bytes 22609920 | tf_op jit(solution)/shard_map/dot_general | solution.py:93
  314.4 0.7 copy-done.7
  315.0 0.1 copy.57
  315.1 0.1 copy.67
  315.2 0.1 reshape.77
  315.4 0.0 copy-done.10
  315.4 8.4 %fusion.2 = bf16[1,4096,384]{2,1,0:T(8,128)(2,1)} fusion(bf16[768,4096]{1,0:T(8,128)(2,1)} %bitcast.88, bf16[768,384]{1,0:T(8,128)(2,1)S(1)} %copy-done.10), kind=kOutput, calls=%fused_computation.9 | convolution fusion | flops 2417491968 | bytes 10027008 | tf_op jit(solution)/shard_map/dot_general | solution.py:82
  323.8 65.4 %reduce-scatter.3.cloned.1.call-done = bf16[768,256]{1,0:T(8,128)(2,1)} async-done(((bf16[768,4096]{1,0:T(8,128)(2,1)}), bf16[768,256]{1,0:T(8,128)(2,1)}) %reduce-scatter.3.cloned.1.call-update) | async-done | bytes 393232 | tf_op jit(solution)/shard_map/reduce_scatter | solution.py:17
  389.3 4.9 all-to-all-start.4
  394.2 7.9 %fusion.1 = bf16[1,4096,384]{2,1,0:T(8,128)(2,1)} fusion(bf16[768,4096]{1,0:T(8,128)(2,1)} %bitcast.84, bf16[768,384]{1,0:T(8,128)(2,1)S(1)} %copy-done.6), kind=kOutput, calls=%fused_computation.8 | convolution fusion | flops 2417491968 | bytes 10027008 | tf_op jit(solution)/shard_map/dot_general | solution.py:88
  402.1 79.6 %reduce-scatter.5.cloned.1.call-done = bf16[768,256]{1,0:T(8,128)(2,1)} async-done(((bf16[768,4096]{1,0:T(8,128)(2,1)}), bf16[768,256]{1,0:T(8,128)(2,1)}) %reduce-scatter.5.cloned.1.call-update) | async-done | bytes 393232 | tf_op jit(solution)/shard_map/reduce_scatter | solution.py:17
  481.7 5.2 %all-to-all-start.6 = ((bf16[8,96,256]{2,1,0:T(8,128)(2,1)}), bf16[8,96,256]{2,1,0:T(8,128)(2,1)S(1)}, u32[]{:S(2)}, u32[]{:S(2)}) async-start(bf16[8,96,256]{2,1,0:T(8,128)(2,1)} %bitcast.81), calls=%async_computation.8 | async-start | bytes 786432 | tf_op jit(solution)/shard_map/all_to_all | solution.py:24
  486.9 8.0 %fusion = bf16[1,4096,384]{2,1,0:T(8,128)(2,1)} fusion(bf16[768,4096]{1,0:T(8,128)(2,1)} %bitcast.85, bf16[768,384]{1,0:T(8,128)(2,1)S(1)} %copy-done.5), kind=kOutput, calls=%fused_computation.7 | convolution fusion | flops 2417491968 | bytes 10027008 | tf_op jit(solution)/shard_map/dot_general | solution.py:85
  494.8 1.1 gather_fusion
  496.0 0.1 reshape.95
  496.1 1.2 gather_fusion.1
  497.3 0.1 reshape.88
  497.3 1.0 multiply_reduce_fusion
  498.4 0.9 reduce_sum.55
  (35 shorter events, 0.3 us)
Async XLA Ops:
  7.2 4.1 copy-start
  7.2 30.3 %copy-start.4 = (bf16[1,256,6144]{2,1,0:T(8,128)(2,1)S(1)}, bf16[1,256,6144]{2,1,0:T(8,128)(2,1)}, u32[]{:S(2)}) copy-start(bf16[1,256,6144]{2,1,0:T(8,128)(2,1)} %param.11) | copy-start | bytes 9437188
  7.2 266.0 %all-gather.3.cloned.1.call-start = ((), (), s32[]{:S(2)}) async-start(), calls=%async_computation.9 | async-start | bytes 6684672 | tf_op jit(solution)/shard_map/all_gather | solution.py:57
  25.1 260.9 %all-gather.5.cloned.1.call-start = ((), (), s32[]{:S(2)}) async-start(), calls=%async_computation.11 | async-start | bytes 6684672 | tf_op jit(solution)/shard_map/all_gather | solution.py:58
  83.5 61.1 %all-to-all-start.1 = ((bf16[16,2,49152]{2,1,0:T(2,128)(2,1)}), bf16[16,2,49152]{2,1,0:T(2,128)(2,1)S(1)}, u32[]{:S(2)}, u32[]{:S(2)}) async-start(bf16[16,2,49152]{2,1,0:T(2,128)(2,1)} %reshape.99), calls=%async_computation.1 | async-start | bytes 6291456 | tf_op jit(solution)/shard_map/all_to_all | solution.py:38
  144.6 61.3 %all-to-all-start.2 = ((bf16[16,2,49152]{2,1,0:T(2,128)(2,1)}), bf16[16,2,49152]{2,1,0:T(2,128)(2,1)}, u32[]{:S(2)}, u32[]{:S(2)}) async-start(bf16[16,2,49152]{2,1,0:T(2,128)(2,1)} %reshape.97), calls=%async_computation.2 | async-start | bytes 6291456 | tf_op jit(solution)/shard_map/all_to_all | solution.py:39
  206.0 49.7 %all-to-all-start.3 = ((bf16[16,2,49152]{2,1,0:T(2,128)(2,1)}), bf16[16,2,49152]{2,1,0:T(2,128)(2,1)}, u32[]{:S(2)}, u32[]{:S(2)}) async-start(bf16[16,2,49152]{2,1,0:T(2,128)(2,1)} %reshape.101), calls=%async_computation.3 | async-start | bytes 6291456 | tf_op jit(solution)/shard_map/all_to_all | solution.py:40
  213.4 175.9 %reduce-scatter.3.cloned.1.call-start = ((), (), s32[]{:S(2)}) async-start(), calls=%async_computation.10 | async-start | bytes 6684672 | tf_op jit(solution)/shard_map/reduce_scatter | solution.py:17
  273.2 8.4 %copy-start.2 = (bf16[1,16,256,384]{3,2,1,0:T(8,128)(2,1)S(1)}, bf16[1,16,256,384]{3,2,1,0:T(8,128)(2,1)}, u32[]{:S(2)}) copy-start(bf16[1,16,256,384]{3,2,1,0:T(8,128)(2,1)} %copy.64) | copy-start | bytes 9437188
  273.2 8.4 %copy-start.8 = (bf16[8,96,4096]{2,1,0:T(8,128)(2,1)S(1)}, bf16[8,96,4096]{2,1,0:T(8,128)(2,1)}, u32[]{:S(2)}) copy-start(bf16[8,96,4096]{2,1,0:T(8,128)(2,1)} %all-gather.3.cloned.1.call-done) | copy-start | bytes 18874372
  281.6 4.4 copy-start.3
  294.2 0.9 copy-start.9
  300.4 1.1 copy-start.5
  300.5 181.2 %reduce-scatter.5.cloned.1.call-start = ((), (), s32[]{:S(2)}) async-start(), calls=%async_computation.12 | async-start | bytes 6684672 | tf_op jit(solution)/shard_map/reduce_scatter | solution.py:17
  301.5 5.4 %copy-start.6 = (bf16[768,384]{1,0:T(8,128)(2,1)S(1)}, bf16[768,384]{1,0:T(8,128)(2,1)}, u32[]{:S(2)}) copy-start(bf16[768,384]{1,0:T(8,128)(2,1)} %get-tuple-element.9) | copy-start | bytes 1769476
  314.3 0.7 copy-start.7
  314.3 1.1 copy-start.10
  389.3 92.4 %all-to-all-start.4 = ((bf16[8,96,256]{2,1,0:T(8,128)(2,1)}), bf16[8,96,256]{2,1,0:T(8,128)(2,1)S(1)}, u32[]{:S(2)}, u32[]{:S(2)}) async-start(bf16[8,96,256]{2,1,0:T(8,128)(2,1)} %bitcast.82), calls=%async_computation.5 | async-start | bytes 786432 | tf_op jit(solution)/shard_map/all_to_all | solution.py:24
  481.7 14.4 %all-to-all-start.6 = ((bf16[8,96,256]{2,1,0:T(8,128)(2,1)}), bf16[8,96,256]{2,1,0:T(8,128)(2,1)S(1)}, u32[]{:S(2)}, u32[]{:S(2)}) async-start(bf16[8,96,256]{2,1,0:T(8,128)(2,1)} %bitcast.81), calls=%async_computation.8 | async-start | bytes 786432 | tf_op jit(solution)/shard_map/all_to_all | solution.py:24
  486.9 12.5 %copy-start.1 = (bf16[128,256]{1,0:T(8,128)(2,1)S(1)}, bf16[128,256]{1,0:T(8,128)(2,1)}, u32[]{:S(2)}) copy-start(bf16[128,256]{1,0:T(8,128)(2,1)} %param.7) | copy-start | bytes 196612
Sparse Core Ops, SparseCore 0:
  25.2 69.5 all-gather.2
  97.1 118.1 all-gather.4
  300.6 88.6 reduce-scatter.2
  393.3 88.3 reduce-scatter.4
where the time goes:
time: 515 us; the launch traced here: 506 us
  waiting for transfers between devices  156 us (30%)
  local copies, waits for them, and re-layouts  111 us (22%)
  other arithmetic  102 us (20%)
  matrix products  64.7 us (13%)
  starting transfers between devices  33.1 us (6%)
  blocking collectives  24.8 us (5%)
  between operations  14.2 us (3%)
    reduce_scatter x2, waiting for transfers between devices, feature_total(): lax.psum_scatter(partial_value.astype(jnp.bfloat16), 'shard', scatter_dim...  145 us
    unnamed x37, local copies, waits for them, and re-layouts  99.2 us
    unnamed x3, other arithmetic  97.9 us
    all_to_all x1, blocking collectives, local(): lax.all_to_all(row_send, 'expert', split_axis=0, concat_axis=0, tiled=True)  13.6 us
    all_to_all x1, blocking collectives, local(): lax.all_to_all(grad_send, 'expert', split_axis=0, concat_axis=0, tiled=True)  11.2 us
    all_to_all x1, waiting for transfers between devices, local(): lax.all_to_all(w_down, 'shard', split_axis=2, concat_axis=1, tiled=True)  10.9 us
  transfers between devices with their start and end apart: 9, of which 3 were waited for; matrix products, arithmetic and copies ran while one was open for 50% of the time, Pallas kernels for 0%

commit v1 on v0

--- a/solution.py
+++ b/solution.py
@@ -37,7 +37,12 @@
     gate_own, up_own, down_own = (
         lax.all_to_all(w_gate, "shard", split_axis=2, concat_axis=1, tiled=True),
         lax.all_to_all(w_up, "shard", split_axis=2, concat_axis=1, tiled=True),
-        lax.all_to_all(w_down, "shard", split_axis=2, concat_axis=1, tiled=True),
+        jnp.concatenate(
+            lax.all_to_all(
+                jnp.stack(jnp.split(w_down, lax.axis_size("shard"), axis=2)), "shard", 0, 0
+            ),
+            axis=1,
+        ),
     )
     gate_own = gate_own[0]
     up_own = up_own[0]

time: 515 us -> 478 us (0.928); the launches traced: 506 us -> 476 us
  other arithmetic: 102 us -> 69 us
  waiting for transfers between devices: 156 us -> 174 us
  local copies, waits for them, and re-layouts: 111 us -> 97.3 us
    unnamed x3 -> x2, other arithmetic: 97.9 us -> 64.7 us
    all_to_all x1, waiting for transfers between devices: 0.01 us -> 27.2 us  [local(): lax.all_to_all(w_up, 'shard', split_axis=2, concat_axis=1, tiled=True)]
    unnamed x37 -> x38, local copies, waits for them, and re-layouts: 99.2 us -> 86.7 us
    all_to_all x1, waiting for transfers between devices: 10.9 us -> 0.01 us  [local(): lax.all_to_all(jnp.stack(jnp.split(w_down, lax.axis_size('shard'), axis=2...]
  transfers between devices with their start and end apart: 9 -> 9, of which waited for: 3 -> 3; matrix products, arithmetic and copies ran while one was open for 50% -> 44% of each run, Pallas kernels for 0% -> 0%
where the time goes in v1:
time: 478 us; the launch traced here: 476 us
  waiting for transfers between devices  174 us (36%)
  local copies, waits for them, and re-layouts  97.3 us (20%)
  other arithmetic  69 us (14%)
  matrix products  64.3 us (13%)
  starting transfers between devices  32.1 us (7%)
  blocking collectives  24.8 us (5%)
  between operations  14 us (3%)
    reduce_scatter x2, waiting for transfers between devices, feature_total(): lax.psum_scatter(partial_value.astype(jnp.bfloat16), 'shard', scatter_dim...  147 us
    unnamed x38, local copies, waits for them, and re-layouts  86.7 us
    unnamed x2, other arithmetic  64.7 us
    all_to_all x1, waiting for transfers between devices, local(): lax.all_to_all(w_up, 'shard', split_axis=2, concat_axis=1, tiled=True)  27.2 us
    all_to_all x1, blocking collectives, local(): lax.all_to_all(row_send, 'expert', split_axis=0, concat_axis=0, tiled=True)  13.6 us
    all_to_all x1, blocking collectives, local(): lax.all_to_all(grad_send, 'expert', split_axis=0, concat_axis=0, tiled=True)  11.2 us
    all_to_all x2, starting transfers between devices, send_home(): lax.all_to_all(shaped, 'expert', split_axis=0, concat_axis=0, tiled=True)  9.79 us
  transfers between devices with their start and end apart: 9, of which 3 were waited for; matrix products, arithmetic and copies ran while one was open for 44% of the time, Pallas kernels for 0%

profile of v1, /device:TPU:2, one launch (start us, length us, event | category | flops | bytes accessed | tf_op | source)
XLA Modules:
  0.0 476.0 jit_solution(10376880306349693636)
XLA Ops:
  7.2 0.9 copy.52
  8.3 0.1 eq.39
  8.5 0.6 reduce-window.6
  9.1 0.2 slice_reduce_fusion
  9.4 0.1 reduce_sum.51
  9.6 0.7 compare_select_fusion
  10.3 0.9 select_reduce_fusion
  11.2 0.2 convolution_convert_fusion.4
  11.5 13.6 %all_to_all.55 = bf16[8,96,256]{2,1,0:T(8,128)(2,1)} all-to-all(bf16[8,96,256]{2,1,0:T(8,128)(2,1)S(1)} %bitcast.102), channel_id=1, replica_groups=mesh['expert'=8,'shard'=16] {'expert'}, dimensions={0} | all-to-all | bytes 786432 | tf_op jit(solution)/shard_map/all_to_all | solution.py:58
  25.2 1.1 fusion.3
  26.2 11.2 %all_to_all.56 = bf16[8,96,256]{2,1,0:T(8,128)(2,1)} all-to-all(bf16[8,96,256]{2,1,0:T(8,128)(2,1)S(1)} %bitcast.101), channel_id=1, replica_groups=mesh['expert'=8,'shard'=16] {'expert'}, dimensions={0} | all-to-all | bytes 786432 | tf_op jit(solution)/shard_map/all_to_all | solution.py:59
  37.5 10.5 %copy.55 = bf16[1,256,6144]{1,0,2:T(2,128)(2,1)} copy(bf16[1,256,6144]{2,1,0:T(8,128)(2,1)S(1)} %copy-done.3) | data formatting | bytes 6291456 | tf_op args[4]
  48.0 0.5 broadcast.52
  48.5 31.5 %reduce.4 = bf16[6144,256]{1,0:T(8,128)(2,1)S(1)} reduce(bf16[6144,1,256]{2,1,0:T(2,128)(2,1)} %bitcast.89, bf16[]{:T(256)} %broadcast.52), dimensions={1}, to_apply=%bitcast.65.reduce_sub_computation | reduce | bytes 6291458
  80.0 3.5 reshape.98
  83.5 7.6 %all-to-all-start.1 = ((bf16[16,2,49152]{2,1,0:T(2,128)(2,1)}), bf16[16,2,49152]{2,1,0:T(2,128)(2,1)S(1)}, u32[]{:S(2)}, u32[]{:S(2)}) async-start(bf16[16,2,49152]{2,1,0:T(2,128)(2,1)} %reshape.98), calls=%async_computation.1 | async-start | bytes 6291456 | tf_op jit(solution)/shard_map/all_to_all | solution.py:38
  91.1 14.0 %copy.57 = bf16[1,256,6144]{1,0,2:T(2,128)(2,1)} copy(bf16[1,256,6144]{2,1,0:T(8,128)(2,1)} %param.12) | data formatting | bytes 6291456 | tf_op args[5]
  105.1 33.2 %reduce.5 = bf16[6144,256]{1,0:T(8,128)(2,1)} reduce(bf16[6144,1,256]{2,1,0:T(2,128)(2,1)} %bitcast.90, bf16[]{:T(256)} %broadcast.52), dimensions={1}, to_apply=%bitcast.63.reduce_sub_computation | reduce | bytes 6291458
  138.3 6.3 %reshape.96 = bf16[16,2,49152]{2,1,0:T(2,128)(2,1)} reshape(bf16[6144,256]{1,0:T(8,128)(2,1)} %reduce.5) | data formatting | bytes 6291456
  144.6 1.6 bitcast_dynamic-update-slice_fusion.15
  146.3 1.6 bitcast_dynamic-update-slice_fusion.14
  147.9 1.6 bitcast_dynamic-update-slice_fusion.13
  149.5 7.3 %all-to-all-start.2 = ((bf16[16,2,49152]{2,1,0:T(2,128)(2,1)}), bf16[16,2,49152]{2,1,0:T(2,128)(2,1)}, u32[]{:S(2)}, u32[]{:S(2)}) async-start(bf16[16,2,49152]{2,1,0:T(2,128)(2,1)} %reshape.96), calls=%async_computation.2 | async-start | bytes 6291456 | tf_op jit(solution)/shard_map/all_to_all | solution.py:39
  156.8 1.6 bitcast_dynamic-update-slice_fusion.12
  158.4 1.6 bitcast_dynamic-update-slice_fusion.11
  160.1 1.6 bitcast_dynamic-update-slice_fusion.10
  161.7 1.6 bitcast_dynamic-update-slice_fusion.9
  163.3 1.6 bitcast_dynamic-update-slice_fusion.8
  164.9 1.6 bitcast_dynamic-update-slice_fusion.7
  166.5 1.6 bitcast_dynamic-update-slice_fusion.6
  168.2 1.6 bitcast_dynamic-update-slice_fusion.5
  169.8 1.6 bitcast_dynamic-update-slice_fusion.4
  171.4 1.6 bitcast_dynamic-update-slice_fusion.3
  173.0 1.6 bitcast_dynamic-update-slice_fusion.2
  174.6 1.6 bitcast_dynamic-update-slice_fusion.1
  176.3 1.6 bitcast_dynamic-update-slice_fusion
  177.9 27.2 %all-to-all-done.2 = bf16[16,2,49152]{2,1,0:T(2,128)(2,1)} async-done(((bf16[16,2,49152]{2,1,0:T(2,128)(2,1)}), bf16[16,2,49152]{2,1,0:T(2,128)(2,1)}, u32[]{:S(2)}, u32[]{:S(2)}) %all-to-all-start.2) | async-done | bytes 3145760 | tf_op jit(solution)/shard_map/all_to_all | solution.py:39
  205.0 6.9 %all-to-all-start.3 = ((bf16[16,1,256,384]{3,2,1,0:T(8,128)(2,1)}), bf16[16,1,256,384]{3,2,1,0:T(8,128)(2,1)}, u32[]{:S(2)}, u32[]{:S(2)}) async-start(bf16[16,1,256,384]{3,2,1,0:T(8,128)(2,1)} %bitcast_dynamic-update-slice_fusion), calls=%async_computation.3 | async-start | bytes 6291456 | tf_op jit(solution)/shard_map/all_to_all | solution.py:41
  212.0 0.2 reduce-scatter.3.cloned.1.call-start
  212.2 7.7 %reshape.99 = bf16[6144,1,256]{2,1,0:T(2,128)(2,1)} reshape(bf16[16,2,49152]{2,1,0:T(2,128)(2,1)S(1)} %all-to-all-done.1) | data formatting | bytes 6291456
  219.9 3.3 copy.60
  223.2 2.8 copy.56
  226.0 11.5 %reshape.97 = bf16[6144,1,256]{2,1,0:T(2,128)(2,1)} reshape(bf16[16,2,49152]{2,1,0:T(2,128)(2,1)} %all-to-all-done.2) | data formatting | bytes 6291456
  237.5 3.3 copy.61
  240.8 2.8 copy.58
  243.6 6.6 %fusion.10 = f32[768,384]{1,0:T(8,128)S(1)} fusion(bf16[768,4096]{1,0:T(8,128)(2,1)} %bitcast.105, bf16[4096,384]{1,0:T(8,128)(2,1)} %bitcast.95), kind=kOutput, calls=%fused_computation.50 | convolution fusion | flops 2415919104 | bytes 10616832 | tf_op jit(solution)/shard_map/dot_general | solution.py:68
  250.2 4.4 fusion.11
  254.6 7.9 %multiply_convert_fusion = (bf16[768,384]{1,0:T(8,128)(2,1)S(1)}, bf16[768,384]{1,0:T(8,128)(2,1)S(1)}, bf16[768,384]{1,0:T(8,128)(2,1)S(1)}) fusion(f32[768,384]{1,0:T(8,128)S(1)} %fusion.10, f32[768,384]{1,0:T(8,128)} %fusion.11, bf16[768,4096]{1,0:T(8,128)(2,1)} %bitcast.109, bf16[4096,384]{1,0:T(8,128)(2,1)} %bitcast.24), kind=kOutput, calls=%fused_computation.13 | convolution fusion | flops 2420342784 | bytes 13565952 | tf_op jit(solution)/shard_map/dot_general | solution.py:81
  262.5 7.2 %convolution_convert_fusion = bf16[768,4096]{1,0:T(8,128)(2,1)} fusion(bf16[768,384]{1,0:T(8,128)(2,1)S(1)} %get-tuple-element.11, bf16[4096,384]{1,0:T(8,128)(2,1)} %bitcast.24), kind=kOutput, calls=%fused_computation.3 | convolution fusion | flops 2419064832 | bytes 10027008 | tf_op jit(solution)/shard_map/dot_general | solution.py:73
  269.7 0.3 reduce-scatter.5.cloned.1.call-start
  270.0 5.3 %fusion.12 = f32[768,4096]{1,0:T(8,128)S(1)} fusion(bf16[768,384]{1,0:T(8,128)(2,1)S(1)} %get-tuple-element.10, bf16[4096,384]{1,0:T(8,128)(2,1)} %bitcast.96), kind=kOutput, calls=%fused_computation.52 | convolution fusion | flops 2415919104 | bytes 16318464 | tf_op jit(solution)/shard_map/dot_general | solution.py:97
  275.4 7.2 %add_convert_fusion = bf16[768,4096]{1,0:T(8,128)(2,1)} fusion(f32[768,4096]{1,0:T(8,128)S(1)} %fusion.12, bf16[768,384]{1,0:T(8,128)(2,1)S(1)} %get-tuple-element.9, bf16[4096,384]{1,0:T(8,128)(2,1)} %bitcast.97), kind=kOutput, calls=%fused_computation.2 | convolution fusion | flops 2422210560 | bytes 22609920 | tf_op jit(solution)/shard_map/dot_general | solution.py:98
  282.6 0.7 copy-done.4
  283.7 8.4 %fusion.2 = bf16[1,4096,384]{2,1,0:T(8,128)(2,1)} fusion(bf16[768,4096]{1,0:T(8,128)(2,1)} %bitcast.110, bf16[768,384]{1,0:T(8,128)(2,1)S(1)} %get-tuple-element.11), kind=kOutput, calls=%fused_computation.9 | convolution fusion | flops 2417491968 | bytes 10027008 | tf_op jit(solution)/shard_map/dot_general | solution.py:87
  292.0 67.6 %reduce-scatter.3.cloned.1.call-done = bf16[768,256]{1,0:T(8,128)(2,1)} async-done(((bf16[768,4096]{1,0:T(8,128)(2,1)}), bf16[768,256]{1,0:T(8,128)(2,1)}) %reduce-scatter.3.cloned.1.call-update) | async-done | bytes 393232 | tf_op jit(solution)/shard_map/reduce_scatter | solution.py:17
  359.6 4.9 %all-to-all-start.4 = ((bf16[8,96,256]{2,1,0:T(8,128)(2,1)}), bf16[8,96,256]{2,1,0:T(8,128)(2,1)S(1)}, u32[]{:S(2)}, u32[]{:S(2)}) async-start(bf16[8,96,256]{2,1,0:T(8,128)(2,1)} %bitcast.104), calls=%async_computation.5 | async-start | bytes 786432 | tf_op jit(solution)/shard_map/all_to_all | solution.py:24
  364.5 7.9 %fusion.1 = bf16[1,4096,384]{2,1,0:T(8,128)(2,1)} fusion(bf16[768,4096]{1,0:T(8,128)(2,1)} %bitcast.106, bf16[768,384]{1,0:T(8,128)(2,1)S(1)} %get-tuple-element.9), kind=kOutput, calls=%fused_computation.8 | convolution fusion | flops 2417491968 | bytes 10027008 | tf_op jit(solution)/shard_map/dot_general | solution.py:93
  372.5 79.6 %reduce-scatter.5.cloned.1.call-done = bf16[768,256]{1,0:T(8,128)(2,1)} async-done(((bf16[768,4096]{1,0:T(8,128)(2,1)}), bf16[768,256]{1,0:T(8,128)(2,1)}) %reduce-scatter.5.cloned.1.call-update) | async-done | bytes 393232 | tf_op jit(solution)/shard_map/reduce_scatter | solution.py:17
  452.1 4.9 %all-to-all-start.6 = ((bf16[8,96,256]{2,1,0:T(8,128)(2,1)}), bf16[8,96,256]{2,1,0:T(8,128)(2,1)S(1)}, u32[]{:S(2)}, u32[]{:S(2)}) async-start(bf16[8,96,256]{2,1,0:T(8,128)(2,1)} %bitcast.103), calls=%async_computation.8 | async-start | bytes 786432 | tf_op jit(solution)/shard_map/all_to_all | solution.py:24
  457.0 8.0 %fusion = bf16[1,4096,384]{2,1,0:T(8,128)(2,1)} fusion(bf16[768,4096]{1,0:T(8,128)(2,1)} %bitcast.107, bf16[768,384]{1,0:T(8,128)(2,1)S(1)} %get-tuple-element.10), kind=kOutput, calls=%fused_computation.7 | convolution fusion | flops 2417491968 | bytes 10027008 | tf_op jit(solution)/shard_map/dot_general | solution.py:90
  464.9 1.1 gather_fusion
  466.2 1.2 gather_fusion.1
  467.5 1.0 multiply_reduce_fusion
  468.5 0.9 reduce_sum.55
  (35 shorter events, 1.1 us)
Async XLA Ops:
  7.2 4.1 copy-start
  7.2 30.3 %copy-start.3 = (bf16[1,256,6144]{2,1,0:T(8,128)(2,1)S(1)}, bf16[1,256,6144]{2,1,0:T(8,128)(2,1)}, u32[]{:S(2)}) copy-start(bf16[1,256,6144]{2,1,0:T(8,128)(2,1)} %param.11) | copy-start | bytes 9437188
  7.2 236.4 %all-gather.3.cloned.1.call-start = ((), (), s32[]{:S(2)}) async-start(), calls=%async_computation.9 | async-start | bytes 6684672 | tf_op jit(solution)/shard_map/all_gather | solution.py:62
  25.1 229.5 %all-gather.5.cloned.1.call-start = ((), (), s32[]{:S(2)}) async-start(), calls=%async_computation.11 | async-start | bytes 6684672 | tf_op jit(solution)/shard_map/all_gather | solution.py:63
  83.5 66.0 %all-to-all-start.1 = ((bf16[16,2,49152]{2,1,0:T(2,128)(2,1)}), bf16[16,2,49152]{2,1,0:T(2,128)(2,1)S(1)}, u32[]{:S(2)}, u32[]{:S(2)}) async-start(bf16[16,2,49152]{2,1,0:T(2,128)(2,1)} %reshape.98), calls=%async_computation.1 | async-start | bytes 6291456 | tf_op jit(solution)/shard_map/all_to_all | solution.py:38
  149.5 55.5 %all-to-all-start.2 = ((bf16[16,2,49152]{2,1,0:T(2,128)(2,1)}), bf16[16,2,49152]{2,1,0:T(2,128)(2,1)}, u32[]{:S(2)}, u32[]{:S(2)}) async-start(bf16[16,2,49152]{2,1,0:T(2,128)(2,1)} %reshape.96), calls=%async_computation.2 | async-start | bytes 6291456 | tf_op jit(solution)/shard_map/all_to_all | solution.py:39
  205.0 49.5 %all-to-all-start.3 = ((bf16[16,1,256,384]{3,2,1,0:T(8,128)(2,1)}), bf16[16,1,256,384]{3,2,1,0:T(8,128)(2,1)}, u32[]{:S(2)}, u32[]{:S(2)}) async-start(bf16[16,1,256,384]{3,2,1,0:T(8,128)(2,1)} %bitcast_dynamic-update-slice_fusion), calls=%async_computation.3 | async-start | bytes 6291456 | tf_op jit(solution)/shard_map/all_to_all | solution.py:41
  212.0 147.7 %reduce-scatter.3.cloned.1.call-start = ((), (), s32[]{:S(2)}) async-start(), calls=%async_computation.10 | async-start | bytes 6684672 | tf_op jit(solution)/shard_map/reduce_scatter | solution.py:17
  243.6 6.6 %copy-start.2 = (bf16[1,16,256,384]{3,2,1,0:T(8,128)(2,1)S(1)}, bf16[1,16,256,384]{3,2,1,0:T(8,128)(2,1)}, u32[]{:S(2)}) copy-start(bf16[1,16,256,384]{3,2,1,0:T(8,128)(2,1)} %copy.58) | copy-start | bytes 9437188
  243.6 6.6 %copy-start.5 = (bf16[8,96,4096]{2,1,0:T(8,128)(2,1)S(1)}, bf16[8,96,4096]{2,1,0:T(8,128)(2,1)}, u32[]{:S(2)}) copy-start(bf16[8,96,4096]{2,1,0:T(8,128)(2,1)} %all-gather.3.cloned.1.call-done) | copy-start | bytes 18874372
  269.7 182.3 %reduce-scatter.5.cloned.1.call-start = ((), (), s32[]{:S(2)}) async-start(), calls=%async_computation.12 | async-start | bytes 6684672 | tf_op jit(solution)/shard_map/reduce_scatter | solution.py:17
  282.6 0.7 copy-start.4
  359.6 92.4 %all-to-all-start.4 = ((bf16[8,96,256]{2,1,0:T(8,128)(2,1)}), bf16[8,96,256]{2,1,0:T(8,128)(2,1)S(1)}, u32[]{:S(2)}, u32[]{:S(2)}) async-start(bf16[8,96,256]{2,1,0:T(8,128)(2,1)} %bitcast.104), calls=%async_computation.5 | async-start | bytes 786432 | tf_op jit(solution)/shard_map/all_to_all | solution.py:24
  452.1 14.1 %all-to-all-start.6 = ((bf16[8,96,256]{2,1,0:T(8,128)(2,1)}), bf16[8,96,256]{2,1,0:T(8,128)(2,1)S(1)}, u32[]{:S(2)}, u32[]{:S(2)}) async-start(bf16[8,96,256]{2,1,0:T(8,128)(2,1)} %bitcast.103), calls=%async_computation.8 | async-start | bytes 786432 | tf_op jit(solution)/shard_map/all_to_all | solution.py:24
  457.0 12.5 %copy-start.1 = (bf16[128,256]{1,0:T(8,128)(2,1)S(1)}, bf16[128,256]{1,0:T(8,128)(2,1)}, u32[]{:S(2)}) copy-start(bf16[128,256]{1,0:T(8,128)(2,1)} %param.7) | copy-start | bytes 196612
Sparse Core Ops, SparseCore 0:
  25.2 69.5 all-gather.2
  97.1 113.2 all-gather.4
  269.9 89.7 reduce-scatter.2
  363.6 88.3 reduce-scatter.4
